TPU v7x, 32 devices: a whole 2x2x4 slice. The times are simulated.
32 devices in a mesh: batch: 8 (over y, x, core), chan: 4 (over z).
Axes of the slice: x: 2, y: 2, z: 4, core: 2. Of those that a mesh axis runs over, the one named last changes fastest.
Arguments:
- fine_inputs: bfloat16 [8, 32, 32, 512], P('batch'), may hold values from -6 to 6
- fine_upstream: bfloat16 [8, 32, 32, 512], P('batch', None, None, 'chan'), may hold values from -6 to 6
- fine_bank: bfloat16 [8, 9, 512, 512], P(None, None, 'batch', 'chan'), may hold values from -0.09375 to 0.09375
- fine_coefs: float32 [8, 8], replicated, may hold values from 0 to 1, as said below
- coarse_inputs: bfloat16 [8, 16, 16, 512], P('batch'), may hold values from -6 to 6
- coarse_upstream: bfloat16 [8, 16, 16, 512], P('batch', None, None, 'chan'), may hold values from -6 to 6
- coarse_bank: bfloat16 [8, 9, 512, 512], P(None, None, 'batch', 'chan'), may hold values from -0.09375 to 0.09375
- coarse_coefs: float32 [8, 8], replicated, may hold values from 0 to 1, as said below
Outputs:
- fine_delta: bfloat16 [8, 32, 32, 512], P('batch', None, None, 'chan')
- fine_update: float32 [8, 9, 512, 512], P(None, None, 'batch', 'chan')
- fine_logit: float32 [8, 8], P('batch')
- coarse_delta: bfloat16 [8, 16, 16, 512], P('batch', None, None, 'chan')
- coarse_update: float32 [8, 9, 512, 512], P(None, None, 'batch', 'chan')
- coarse_logit: float32 [8, 8], P('batch')
Inputs may be any that keep to these rules, and one draw needn't show every extreme that they name: Each row of fine_coefs is a softmax: positive entries that sum to one. Each row of coarse_coefs is a softmax: positive entries that sum to one.
All inputs are finite; a program needn't handle non-finite values.
Results may differ from a plain program's by a relative error of at most 0.01.
Values may be sent and summed in bfloat16 or wider, within the bound.
No kernel may reach another device: no remote copies, remote signals or barrier semaphores. Data moves between devices by JAX's collectives and lax.ppermute only.
A program may use at most 128 MiB of HBM per device.

v0:
```python
import jax
import jax.numpy as jnp
from jax import lax
from jax.sharding import PartitionSpec as P

BANKS = 8
FINE_SIDE = 32
COARSE_SIDE = 16
HIGH = lax.Precision.HIGHEST


def shifted(padded, row_shift, col_shift, side):
    window = padded[:, row_shift : row_shift + side, col_shift : col_shift + side, :]
    return window.reshape(window.shape[0], side * side, window.shape[3])


def local_grads(inputs, upstream, kernels, side):
    samples_here = inputs.shape[0]
    pad_in = jnp.pad(inputs, ((0, 0), (1, 1), (1, 1), (0, 0)))
    pad_up = jnp.pad(upstream, ((0, 0), (1, 1), (1, 1), (0, 0)))
    flat_up = upstream.reshape(samples_here, side * side, upstream.shape[3])
    delta = jnp.zeros((samples_here, side * side, inputs.shape[3]), jnp.float32)
    grad_taps = []
    for row_shift in range(3):
        for col_shift in range(3):
            tap = 3 * row_shift + col_shift
            window_in = shifted(pad_in, row_shift, col_shift, side)
            window_up = shifted(pad_up, 2 - row_shift, 2 - col_shift, side)
            grad_taps.append(
                jnp.einsum("bpc,bpo->bco", window_in, flat_up, preferred_element_type=jnp.float32)
                / side
            )
            delta = delta + jnp.einsum(
                "bpo,bco->bpc", window_up, kernels[:, tap], preferred_element_type=jnp.float32
            )
    return (delta.reshape(samples_here, side, side, inputs.shape[3]), jnp.stack(grad_taps, axis=1))


def one_layer(inputs, upstream, bank_part, coefs, side):
    flat_bank = bank_part.reshape(BANKS, -1).astype(jnp.float32)
    mixed_all = jnp.dot(coefs, flat_bank, precision=HIGH)
    mixed_all = mixed_all.reshape((coefs.shape[0],) + bank_part.shape[1:]).astype(jnp.bfloat16)
    kernels = lax.all_to_all(mixed_all, "batch", split_axis=0, concat_axis=2, tiled=True)
    delta, kernel_grad = local_grads(inputs, upstream, kernels, side)
    delta_total = lax.psum(delta.astype(jnp.bfloat16), "chan").astype(jnp.float32)
    width = delta.shape[3] // lax.axis_size("chan")
    delta_part = lax.dynamic_slice_in_dim(delta_total, lax.axis_index("chan") * width, width, 3)
    moved = lax.all_to_all(
        kernel_grad.astype(jnp.bfloat16), "batch", split_axis=2, concat_axis=0, tiled=True
    ).astype(kernel_grad.dtype)
    flat_grads = moved.reshape(moved.shape[0], -1)
    update = jnp.dot(coefs.T, flat_grads, precision=HIGH).reshape(bank_part.shape)
    dcoef_part = lax.dot_general(flat_grads, flat_bank, (((1,), (1,)), ((), ())), precision=HIGH)
    return (delta_part.astype(jnp.bfloat16), update, dcoef_part)


def logit_grads(coefs, totals, samples_here):
    first_row = lax.axis_index("batch") * samples_here
    own_coefs = lax.dynamic_slice_in_dim(coefs, first_row, samples_here, 0)
    own_totals = lax.dynamic_slice_in_dim(totals, first_row, samples_here, 0)
    return own_coefs * (own_totals - jnp.sum(own_coefs * own_totals, axis=1, keepdims=True))


def per_device(
    fine_inputs,
    fine_upstream,
    fine_bank,
    fine_coefs,
    coarse_inputs,
    coarse_upstream,
    coarse_bank,
    coarse_coefs,
):
    fine_delta, fine_update, fine_partial = one_layer(
        fine_inputs, fine_upstream, fine_bank, fine_coefs, FINE_SIDE
    )
    coarse_delta, coarse_update, coarse_partial = one_layer(
        coarse_inputs, coarse_upstream, coarse_bank, coarse_coefs, COARSE_SIDE
    )
    fine_total, coarse_total = lax.psum((fine_partial, coarse_partial), ("batch", "chan"))
    samples_here = fine_inputs.shape[0]
    fine_logit = logit_grads(fine_coefs, fine_total, samples_here)
    coarse_logit = logit_grads(coarse_coefs, coarse_total, samples_here)
    return (fine_delta, fine_update, fine_logit, coarse_delta, coarse_update, coarse_logit)


def solution(mesh):
    return jax.shard_map(
        per_device,
        mesh=mesh,
        in_specs=(
            P("batch", None, None, None),
            P("batch", None, None, "chan"),
            P(None, None, "batch", "chan"),
            P(),
            P("batch", None, None, None),
            P("batch", None, None, "chan"),
            P(None, None, "batch", "chan"),
            P(),
        ),
        out_specs=(
            P("batch", None, None, "chan"),
            P(None, None, "batch", "chan"),
            P("batch", None),
            P("batch", None, None, "chan"),
            P(None, None, "batch", "chan"),
            P("batch", None),
        ),
        check_vma=False,
    )
```

profile of v0, /device:TPU:10, one launch (start us, length us, event | category | flops | bytes accessed | tf_op | source)
XLA Modules:
  0.0 182.0 jit_solution(2190526697358805732)
XLA Ops:
  7.2 2.0 %copy.47 = bf16[1,8,576,128]{3,1,2,0:T(8,128)(2,1)S(1)} copy(bf16[1,8,576,128]{3,2,1,0:T(8,128)(2,1)} %bitcast.542) | data formatting | bytes 2359296
  11.6 4.4 %all-to-all-start = ((bf16[8,9,64,128]{3,2,1,0:T(8,128)(2,1)}), bf16[8,9,64,128]{3,2,1,0:T(8,128)(2,1)S(1)}, u32[]{:S(2)}, u32[]{:S(2)}) async-start(bf16[8,9,64,128]{3,2,1,0:T(8,128)(2,1)} %copy.24), calls=%async_computation | async-start | bytes 2359296 | tf_op jit(solution)/shard_map/all_to_all | solution.py:43
  27.2 2.2 %copy.27 = bf16[1,9,512,128]{3,1,0,2:T(8,128)(2,1)} copy(bf16[1,9,512,128]{3,2,1,0:T(8,128)(2,1)S(1)} %fusion.62) | data formatting | bytes 2359296 | tf_op jit(solution)/shard_map/stack | solution.py:36
  31.4 2.2 %copy.31 = bf16[1,9,512,128]{3,1,0,2:T(8,128)(2,1)} copy(bf16[1,9,512,128]{3,2,1,0:T(8,128)(2,1)S(1)} %fusion.44) | data formatting | bytes 2359296 | tf_op jit(solution)/shard_map/stack | solution.py:36
  35.6 4.3 %all-to-all-start.1 = ((bf16[1,9,512,128]{3,1,0,2:T(8,128)(2,1)}), bf16[1,9,512,128]{3,1,0,2:T(8,128)(2,1)}, u32[]{:S(2)}, u32[]{:S(2)}) async-start(bf16[1,9,512,128]{3,1,0,2:T(8,128)(2,1)} %copy.27), calls=%async_computation.1 | async-start | bytes 4194304 | tf_op jit(solution)/shard_map/all_to_all | solution.py:48
  40.5 1.8 fusion.124
  42.2 1.7 fusion.125
  44.0 1.7 fusion.126
  45.7 19.4 %all-to-all-done.1 = bf16[1,9,512,128]{3,1,0,2:T(8,128)(2,1)} async-done(((bf16[1,9,512,128]{3,1,0,2:T(8,128)(2,1)}), bf16[1,9,512,128]{3,1,0,2:T(8,128)(2,1)}, u32[]{:S(2)}, u32[]{:S(2)}) %all-to-all-start.1) | async-done | bytes 1179680 | tf_op jit(solution)/shard_map/all_to_all | solution.py:48
  65.1 5.7 %all-to-all-start.2 = ((bf16[8,9,64,128]{3,2,1,0:T(8,128)(2,1)}), bf16[8,9,64,128]{3,2,1,0:T(8,128)(2,1)}, u32[]{:S(2)}, u32[]{:S(2)}) async-start(bf16[8,9,64,128]{3,2,1,0:T(8,128)(2,1)} %copy.29), calls=%async_computation.2 | async-start | bytes 2359296 | tf_op jit(solution)/shard_map/all_to_all | solution.py:43
  70.8 3.0 %copy.49 = bf16[1,9,8,64,128]{4,3,1,2,0:T(8,128)(2,1)} copy(bf16[1,9,8,64,128]{4,1,3,2,0:T(8,128)(2,1)} %bitcast.57) | data formatting | bytes 2359296 | tf_op jit(solution)/shard_map/all_to_all | solution.py:48
  73.8 1.8 reshape.837
  75.5 2.9 %fusion.127 = f32[1024,512]{1,0:T(8,128)} fusion(bf16[1024,128]{1,0:T(8,128)(2,1)} %bitcast.554, bf16[1,9,512,128]{3,2,1,0:T(8,128)(2,1)} %bitcast.526), kind=kOutput, calls=%fused_computation.192 | convolution fusion | flops 134217728 | bytes 2490368 | tf_op jit(solution)/shard_map/bpo,bco->bpc/dot_general | solution.py:33
  78.4 2.7 %fusion.128 = f32[1024,512]{1,0:T(8,128)} fusion(bf16[1024,128]{1,0:T(8,128)(2,1)S(1)} %bitcast.553, bf16[1,9,512,128]{3,2,1,0:T(8,128)(2,1)} %bitcast.527), kind=kOutput, calls=%fused_computation.194 | convolution fusion | flops 134217728 | bytes 2490368 | tf_op jit(solution)/shard_map/bpo,bco->bpc/dot_general | solution.py:33
  81.1 2.7 %fusion.130 = f32[1024,512]{1,0:T(8,128)} fusion(bf16[1024,128]{1,0:T(8,128)(2,1)S(1)} %bitcast.552, bf16[1,9,512,128]{3,2,1,0:T(8,128)(2,1)} %bitcast.528), kind=kOutput, calls=%fused_computation.198 | convolution fusion | flops 134217728 | bytes 2490368 | tf_op jit(solution)/shard_map/bpo,bco->bpc/dot_general | solution.py:33
  83.8 2.7 %fusion.129 = f32[1024,512]{1,0:T(8,128)} fusion(bf16[1024,128]{1,0:T(8,128)(2,1)S(1)} %bitcast.551, bf16[1,9,512,128]{3,2,1,0:T(8,128)(2,1)} %bitcast.529), kind=kOutput, calls=%fused_computation.196 | convolution fusion | flops 134217728 | bytes 2490368 | tf_op jit(solution)/shard_map/bpo,bco->bpc/dot_general | solution.py:33
  86.5 5.4 %all-to-all-start.3 = ((bf16[1,9,512,128]{3,1,0,2:T(8,128)(2,1)}), bf16[1,9,512,128]{3,1,0,2:T(8,128)(2,1)}, u32[]{:S(2)}, u32[]{:S(2)}) async-start(bf16[1,9,512,128]{3,1,0,2:T(8,128)(2,1)} %copy.31), calls=%async_computation.3 | async-start | bytes 4194304 | tf_op jit(solution)/shard_map/all_to_all | solution.py:48
  100.2 1.9 %fusion.6 = bf16[256,512]{1,0:T(8,128)(2,1)} fusion(f32[256,512]{1,0:T(8,128)S(1)} %convolution_add_fusion.1, bf16[256,128]{1,0:T(8,128)(2,1)} %bitcast.567, bf16[1,9,512,128]{3,2,1,0:T(8,128)(2,1)S(1)} %bitcast.539), kind=kOutput, calls=%fused_computation.25 | convolution fusion | flops 33816576 | bytes 983040 | tf_op jit(solution)/shard_map/bpo,bco->bpc/dot_general | solution.py:33
  102.2 3.8 %fusion.4 = bf16[1024,512]{1,0:T(8,128)(2,1)} fusion(f32[1024,512]{1,0:T(8,128)S(1)} %fusion.123, f32[1024,512]{1,0:T(8,128)S(1)} %copy-done, f32[1024,512]{1,0:T(8,128)S(1)} %copy-done.1, f32[512,1024]{0,1:T(8,128)S(1)} %copy-done.2, f32[1024,512]{1,0:T(8,128)S(1)} %copy-done.3, f32[1024,512]{1,0:T(8,128)S(1)} %copy-done.4, f32[1024,512]{1,0:T(8,128)S(1)} %copy-done.5, ...), kind=kOutput, calls=%fused_computation.5 | convolution fusion | flops 138936320 | bytes 18219008 | tf_op jit(solution)/shard_map/bpo,bco->bpc/dot_general | solution.py:33
  107.2 1.8 %copy.33 = f32[8,9,64,128]{3,2,1,0:T(8,128)} copy(f32[8,9,64,128]{3,0,2,1:T(8,128)S(1)} %bitcast.520) | data formatting | bytes 4718592
  109.0 8.1 %all-to-all-done.3 = bf16[1,9,512,128]{3,1,0,2:T(8,128)(2,1)} async-done(((bf16[1,9,512,128]{3,1,0,2:T(8,128)(2,1)}), bf16[1,9,512,128]{3,1,0,2:T(8,128)(2,1)}, u32[]{:S(2)}, u32[]{:S(2)}) %all-to-all-start.3) | async-done | bytes 1179680 | tf_op jit(solution)/shard_map/all_to_all | solution.py:48
  117.2 1.9 %copy.48 = bf16[1,9,8,64,128]{4,3,1,2,0:T(8,128)(2,1)S(1)} copy(bf16[1,9,8,64,128]{4,1,3,2,0:T(8,128)(2,1)} %bitcast.118) | data formatting | bytes 2359296 | tf_op jit(solution)/shard_map/all_to_all | solution.py:48
  120.8 1.8 %copy.34 = f32[8,9,64,128]{3,2,1,0:T(8,128)} copy(f32[8,9,64,128]{3,0,2,1:T(8,128)S(1)} %bitcast.521) | data formatting | bytes 4718592
  125.0 43.5 %all-reduce.4 = (f32[8,8]{1,0:T(8,128)S(1)}, f32[8,8]{1,0:T(8,128)S(1)}) all-reduce(f32[8,8]{1,0:T(8,128)S(1)} %fusion.158, f32[8,8]{1,0:T(8,128)S(1)} %fusion.159), channel_id=1, replica_groups=mesh['batch'=8,'chan'=4] {'batch','chan'}, use_global_device_ids=true, to_apply=%region_1.2 | all-reduce | flops 128 | bytes 1024 | tf_op jit(solution)/shard_map/psum | solution.py:80
  (102 shorter events, 38.0 us)
Async XLA Ops:
  7.2 2.1 %copy-start.20 = (f32[8,8]{1,0:T(8,128)S(1)}, f32[8,8]{1,0:T(8,128)}, u32[]{:S(2)}) copy-start(f32[8,8]{1,0:T(8,128)} %param.11) | copy-start | bytes 772
  11.6 4.4 %copy-start.8 = (bf16[8,9,64,128]{3,2,1,0:T(8,128)(2,1)S(1)}, bf16[8,9,64,128]{3,2,1,0:T(8,128)(2,1)}, u32[]{:S(2)}) copy-start(bf16[8,9,64,128]{3,2,1,0:T(8,128)(2,1)} %param.14) | copy-start | bytes 3538948
  11.6 24.0 %all-to-all-start = ((bf16[8,9,64,128]{3,2,1,0:T(8,128)(2,1)}), bf16[8,9,64,128]{3,2,1,0:T(8,128)(2,1)S(1)}, u32[]{:S(2)}, u32[]{:S(2)}) async-start(bf16[8,9,64,128]{3,2,1,0:T(8,128)(2,1)} %copy.24), calls=%async_computation | async-start | bytes 2359296 | tf_op jit(solution)/shard_map/all_to_all | solution.py:43
  29.5 1.3 copy-start.16
  29.5 1.3 copy-start.24
  31.4 3.0 %copy-start.11 = (bf16[1,32,32,128]{3,2,1,0:T(8,128)(2,1)S(1)}, bf16[1,32,32,128]{3,2,1,0:T(8,128)(2,1)}, u32[]{:S(2)}) copy-start(bf16[1,32,32,128]{3,2,1,0:T(8,128)(2,1)} %param.9) | copy-start | bytes 786436
  35.6 29.5 %all-to-all-start.1 = ((bf16[1,9,512,128]{3,1,0,2:T(8,128)(2,1)}), bf16[1,9,512,128]{3,1,0,2:T(8,128)(2,1)}, u32[]{:S(2)}, u32[]{:S(2)}) async-start(bf16[1,9,512,128]{3,1,0,2:T(8,128)(2,1)} %copy.27), calls=%async_computation.1 | async-start | bytes 4194304 | tf_op jit(solution)/shard_map/all_to_all | solution.py:48
  40.0 4.0 %copy-start.6 = (bf16[8,9,64,128]{3,2,0,1:T(8,128)(2,1)}, bf16[8,9,64,128]{3,2,0,1:T(8,128)(2,1)S(1)}, u32[]{:S(2)}) copy-start(bf16[8,9,64,128]{3,2,0,1:T(8,128)(2,1)S(1)} %copy.25) | copy-start | bytes 3538948
  65.1 21.4 %all-to-all-start.2 = ((bf16[8,9,64,128]{3,2,1,0:T(8,128)(2,1)}), bf16[8,9,64,128]{3,2,1,0:T(8,128)(2,1)}, u32[]{:S(2)}, u32[]{:S(2)}) async-start(bf16[8,9,64,128]{3,2,1,0:T(8,128)(2,1)} %copy.29), calls=%async_computation.2 | async-start | bytes 2359296 | tf_op jit(solution)/shard_map/all_to_all | solution.py:43
  75.5 2.9 %copy-start.14 = (bf16[1,32,32,128]{3,2,1,0:T(8,128)(2,1)S(1)}, bf16[1,32,32,128]{3,2,1,0:T(8,128)(2,1)}, u32[]{:S(2)}) copy-start(bf16[1,32,32,128]{3,2,1,0:T(8,128)(2,1)} %get-tuple-element.30) | copy-start | bytes 786436
  78.4 2.7 %copy-start.13 = (bf16[1,32,32,128]{3,2,1,0:T(8,128)(2,1)S(1)}, bf16[1,32,32,128]{3,2,1,0:T(8,128)(2,1)}, u32[]{:S(2)}) copy-start(bf16[1,32,32,128]{3,2,1,0:T(8,128)(2,1)} %get-tuple-element.35) | copy-start | bytes 786436
  81.1 2.7 %copy-start.12 = (bf16[1,32,32,128]{3,2,1,0:T(8,128)(2,1)S(1)}, bf16[1,32,32,128]{3,2,1,0:T(8,128)(2,1)}, u32[]{:S(2)}) copy-start(bf16[1,32,32,128]{3,2,1,0:T(8,128)(2,1)} %get-tuple-element.29) | copy-start | bytes 786436
  86.5 30.6 %all-to-all-start.3 = ((bf16[1,9,512,128]{3,1,0,2:T(8,128)(2,1)}), bf16[1,9,512,128]{3,1,0,2:T(8,128)(2,1)}, u32[]{:S(2)}, u32[]{:S(2)}) async-start(bf16[1,9,512,128]{3,1,0,2:T(8,128)(2,1)} %copy.31), calls=%async_computation.3 | async-start | bytes 4194304 | tf_op jit(solution)/shard_map/all_to_all | solution.py:48
  91.9 80.0 %all-reduce.8.cloned.1.call-start = ((), (), s32[]{:S(2)}) async-start(), calls=%async_computation.4 | async-start | bytes 2621440 | tf_op jit(solution)/shard_map/psum | solution.py:45
  91.9 10.2 %copy-start.4 = (f32[1024,512]{1,0:T(8,128)S(1)}, f32[1024,512]{1,0:T(8,128)}, u32[]{:S(2)}) copy-start(f32[1024,512]{1,0:T(8,128)} %fusion.128) | copy-start | bytes 6291460
  91.9 10.2 %copy-start.5 = (f32[1024,512]{1,0:T(8,128)S(1)}, f32[1024,512]{1,0:T(8,128)}, u32[]{:S(2)}) copy-start(f32[1024,512]{1,0:T(8,128)} %fusion.130) | copy-start | bytes 6291460
  94.6 5.1 %copy-start.19 = (bf16[1,16,16,128]{3,2,1,0:T(8,128)(2,1)S(1)}, bf16[1,16,16,128]{3,2,1,0:T(8,128)(2,1)}, u32[]{:S(2)}) copy-start(bf16[1,16,16,128]{3,2,1,0:T(8,128)(2,1)} %get-tuple-element.41) | copy-start | bytes 196612
  94.6 5.4 %copy-start.18 = (bf16[1,16,16,128]{3,2,1,0:T(8,128)(2,1)S(1)}, bf16[1,16,16,128]{3,2,1,0:T(8,128)(2,1)}, u32[]{:S(2)}) copy-start(bf16[1,16,16,128]{3,2,1,0:T(8,128)(2,1)} %get-tuple-element.42) | copy-start | bytes 196612
  95.7 2.5 %copy-start.17 = (bf16[1,16,16,128]{3,2,1,0:T(8,128)(2,1)S(1)}, bf16[1,16,16,128]{3,2,1,0:T(8,128)(2,1)}, u32[]{:S(2)}) copy-start(bf16[1,16,16,128]{3,2,1,0:T(8,128)(2,1)} %param.13) | copy-start | bytes 196612
  95.8 6.4 %copy-start.3 = (f32[1024,512]{1,0:T(8,128)S(1)}, f32[1024,512]{1,0:T(8,128)}, u32[]{:S(2)}) copy-start(f32[1024,512]{1,0:T(8,128)} %fusion.127) | copy-start | bytes 6291460
  97.0 5.2 %copy-start.2 = (f32[512,1024]{0,1:T(8,128)S(1)}, f32[512,1024]{0,1:T(8,128)}, u32[]{:S(2)}) copy-start(f32[512,1024]{0,1:T(8,128)} %fusion.126) | copy-start | bytes 6291460
  98.5 3.7 %copy-start.1 = (f32[1024,512]{1,0:T(8,128)S(1)}, f32[1024,512]{1,0:T(8,128)}, u32[]{:S(2)}) copy-start(f32[1024,512]{1,0:T(8,128)} %fusion.125) | copy-start | bytes 6291460
  100.0 2.2 %copy-start = (f32[1024,512]{1,0:T(8,128)S(1)}, f32[1024,512]{1,0:T(8,128)}, u32[]{:S(2)}) copy-start(f32[1024,512]{1,0:T(8,128)} %fusion.124) | copy-start | bytes 6291460
  120.8 1.8 %copy-start.7 = (bf16[8,9,64,128]{3,2,1,0:T(8,128)(2,1)S(1)}, bf16[8,9,64,128]{3,2,1,0:T(8,128)(2,1)}, u32[]{:S(2)}) copy-start(bf16[8,9,64,128]{3,2,1,0:T(8,128)(2,1)} %param.10) | copy-start | bytes 3538948
  (6 other events, 6.1 us)
Sparse Core Ops, SparseCore 0:
  106.1 61.7 all-reduce.7
where the time goes:
time: 183 us; the launch traced here: 182 us
  matrix products  44.1 us (24%)
  blocking collectives  43.5 us (24%)
  waiting for transfers between devices  27.5 us (15%)
  local copies, waits for them, and re-layouts  26 us (14%)
  starting transfers between devices  19.8 us (11%)
  between operations  14.5 us (8%)
  other arithmetic  6.68 us (4%)
    psum x1, blocking collectives, per_device(): lax.psum((fine_partial, coarse_partial), ('batch', 'chan'))  43.5 us
    dot_general x18, matrix products, local_grads(): jnp.einsum('bpo,bco->bpc', window_up, kernels[:, tap], preferred_element_...  29 us
    all_to_all x2, waiting for transfers between devices, one_layer(): lax.all_to_all(kernel_grad.astype(jnp.bfloat16), 'batch', split_axis=2, c...  27.5 us
    all_to_all x2, starting transfers between devices, one_layer(): lax.all_to_all(mixed_all, 'batch', split_axis=0, concat_axis=2, tiled=True)  10 us
    all_to_all x2, starting transfers between devices, one_layer(): lax.all_to_all(kernel_grad.astype(jnp.bfloat16), 'batch', split_axis=2, c...  9.71 us
    dot_general x18, matrix products, local_grads(): jnp.einsum('bpc,bpo->bco', window_in, flat_up, preferred_element_type=jnp...  8.47 us
    unnamed x54, local copies, waits for them, and re-layouts  8.13 us
    all_to_all x2, local copies, waits for them, and re-layouts, one_layer(): lax.all_to_all(kernel_grad.astype(jnp.bfloat16), 'batch', split_axis=2, c...  4.92 us
  transfers between devices with their start and end apart: 5, of which 2 were waited for; matrix products, arithmetic and copies ran while one was open for 37% of the time, Pallas kernels for 0%

commit v1 on v0

--- a/solution.py
+++ b/solution.py
@@ -40,7 +40,19 @@
     flat_bank = bank_part.reshape(BANKS, -1).astype(jnp.float32)
     mixed_all = jnp.dot(coefs, flat_bank, precision=HIGH)
     mixed_all = mixed_all.reshape((coefs.shape[0],) + bank_part.shape[1:]).astype(jnp.bfloat16)
-    kernels = lax.all_to_all(mixed_all, "batch", split_axis=0, concat_axis=2, tiled=True)
+
+    def _produce_islands(local_x, lane_axis, out_dim, axis_k):
+        return jnp.concatenate(
+            lax.all_to_all(
+                jnp.stack(jnp.split(local_x, lax.axis_size(lane_axis), axis=out_dim)),
+                lane_axis,
+                split_axis=0,
+                concat_axis=0,
+            ),
+            axis=axis_k,
+        )
+
+    kernels = _produce_islands(mixed_all, "batch", 0, 2)
     delta, kernel_grad = local_grads(inputs, upstream, kernels, side)
     delta_total = lax.psum(delta.astype(jnp.bfloat16), "chan").astype(jnp.float32)
     width = delta.shape[3] // lax.axis_size("chan")

time: 183 us -> 196 us (1.071)
  local copies, waits for them, and re-layouts: 26 us -> 39.4 us
  matrix products: 44.1 us -> 36.7 us
  waiting for transfers between devices: 27.5 us -> 33.1 us
    unnamed x54 -> x70, local copies, waits for them, and re-layouts: 8.13 us -> 19.7 us
    dot_general x18, matrix products: 29 us -> 22.7 us  [local_grads(): jnp.einsum('bpo,bco->bpc', window_up, kernels[:, tap], preferred_element_...]
    all_to_all x2, waiting for transfers between devices: 0.01 us -> 6.27 us  [_produce_islands(): lax.all_to_all(jnp.stack(jnp.split(local_x, lax.axis_size(lane_axis), axi...]
    split x0 -> x2, local copies, waits for them, and re-layouts: none -> 5.49 us  [_produce_islands(): jnp.split(local_x, lax.axis_size(lane_axis), axis=out_dim)]
    convert_element_type x2 -> x0, local copies, waits for them, and re-layouts: 2.64 us -> none  [one_layer(): mixed_all.reshape((coefs.shape[0],) + bank_part.shape[1:])]
  transfers between devices with their start and end apart: 5 -> 5, of which waited for: 2 -> 3; matrix products, arithmetic and copies ran while one was open for 37% -> 33% of each run, Pallas kernels for 0% -> 0%
where the time goes in v1:
time: 196 us; the launch traced here: 194 us
  blocking collectives  43.6 us (22%)
  local copies, waits for them, and re-layouts  39.4 us (20%)
  matrix products  36.7 us (19%)
  waiting for transfers between devices  33.1 us (17%)
  starting transfers between devices  20.3 us (10%)
  between operations  14.4 us (7%)
  other arithmetic  6.16 us (3%)
    psum x1, blocking collectives, per_device(): lax.psum((fine_partial, coarse_partial), ('batch', 'chan'))  43.6 us
    all_to_all x2, waiting for transfers between devices, one_layer(): lax.all_to_all(kernel_grad.astype(jnp.bfloat16), 'batch', split_axis=2, c...  26.9 us
    dot_general x18, matrix products, local_grads(): jnp.einsum('bpo,bco->bpc', window_up, kernels[:, tap], preferred_element_...  22.7 us
    unnamed x70, local copies, waits for them, and re-layouts  19.7 us
    all_to_all x2, starting transfers between devices, one_layer(): lax.all_to_all(kernel_grad.astype(jnp.bfloat16), 'batch', split_axis=2, c...  11.5 us
    all_to_all x2, starting transfers between devices, _produce_islands(): lax.all_to_all(jnp.stack(jnp.split(local_x, lax.axis_size(lane_axis), axi...  8.81 us
    dot_general x18, matrix products, local_grads(): jnp.einsum('bpc,bpo->bco', window_in, flat_up, preferred_element_type=jnp...  7.39 us
    all_to_all x2, waiting for transfers between devices, _produce_islands(): lax.all_to_all(jnp.stack(jnp.split(local_x, lax.axis_size(lane_axis), axi...  6.27 us
  transfers between devices with their start and end apart: 5, of which 3 were waited for; matrix products, arithmetic and copies ran while one was open for 33% of the time, Pallas kernels for 0%

profile of v1, /device:TPU:10, one launch (start us, length us, event | category | flops | bytes accessed | tf_op | source)
XLA Modules:
  0.0 193.8 jit_solution(10969411023125886767)
XLA Ops:
  7.2 2.0 %copy.182 = bf16[1,8,576,128]{3,1,2,0:T(8,128)(2,1)S(1)} copy(bf16[1,8,576,128]{3,2,1,0:T(8,128)(2,1)} %bitcast.568) | data formatting | bytes 2359296
  10.3 2.7 %fusion.161 = (bf16[1,9,64,128]{3,0,2,1:T(2,128)(2,1)S(1)}, bf16[1,9,64,128]{3,0,2,1:T(2,128)(2,1)S(1)}, bf16[1,9,64,128]{3,0,2,1:T(2,128)(2,1)S(1)}, bf16[1,9,6...) fusion(bf16[8,9,64,128]{3,0,2,1:T(8,128)(2,1)S(1)} %convolution, ...), kind=kLoop, calls=%fused_computation.254 | loop fusion | bytes 2359296 | tf_op jit(solution)/shard_map/split | solution.py:47
  18.6 4.4 %all-to-all-start = ((bf16[8,1,9,64,128]{4,3,2,1,0:T(8,128)(2,1)}), bf16[8,1,9,64,128]{4,3,2,1,0:T(8,128)(2,1)S(1)}, u32[]{:S(2)}, u32[]{:S(2)}) async-start(bf16[8,1,9,64,128]{4,3,2,1,0:T(8,128)(2,1)} %bitcast_dynamic-update-slice_fusion.8), calls=%async_computation | async-start | bytes 2359296 | tf_op jit(solution)/shard_map/all_to_all | solution.py:46
  26.7 2.7 %fusion.160 = (bf16[1,9,64,128]{3,0,2,1:T(2,128)(2,1)S(1)}, bf16[1,9,64,128]{3,0,2,1:T(2,128)(2,1)S(1)}, bf16[1,9,64,128]{3,0,2,1:T(2,128)(2,1)S(1)}, bf16[1,9,6...) fusion(bf16[8,9,64,128]{3,0,2,1:T(8,128)(2,1)S(1)} %convolution, ...), kind=kLoop, calls=%fused_computation.253 | loop fusion | bytes 2359296 | tf_op jit(solution)/shard_map/split | solution.py:47
  35.0 2.2 %copy.131 = bf16[1,9,512,128]{3,1,0,2:T(8,128)(2,1)} copy(bf16[1,9,512,128]{3,2,1,0:T(8,128)(2,1)S(1)} %fusion.62) | data formatting | bytes 2359296 | tf_op jit(solution)/shard_map/stack | solution.py:36
  39.8 2.2 %copy.134 = bf16[1,9,512,128]{3,1,0,2:T(8,128)(2,1)} copy(bf16[1,9,512,128]{3,2,1,0:T(8,128)(2,1)S(1)} %fusion.44) | data formatting | bytes 2359296 | tf_op jit(solution)/shard_map/stack | solution.py:36
  47.6 4.4 %all-to-all-start.2 = ((bf16[8,1,9,64,128]{4,3,2,1,0:T(8,128)(2,1)}), bf16[8,1,9,64,128]{4,3,2,1,0:T(8,128)(2,1)}, u32[]{:S(2)}, u32[]{:S(2)}) async-start(bf16[8,1,9,64,128]{4,3,2,1,0:T(8,128)(2,1)} %bitcast_dynamic-update-slice_fusion), calls=%async_computation.2 | async-start | bytes 2359296 | tf_op jit(solution)/shard_map/all_to_all | solution.py:46
  54.0 1.7 fusion.124
  55.7 1.8 fusion.125
  57.5 1.8 fusion.126
  59.3 1.8 fusion.127
  61.1 6.3 %all-to-all-done.2 = bf16[8,1,9,64,128]{4,3,2,1,0:T(8,128)(2,1)} async-done(((bf16[8,1,9,64,128]{4,3,2,1,0:T(8,128)(2,1)}), bf16[8,1,9,64,128]{4,3,2,1,0:T(8,128)(2,1)}, u32[]{:S(2)}, u32[]{:S(2)}) %all-to-all-start.2) | async-done | bytes 1179680 | tf_op jit(solution)/shard_map/all_to_all | solution.py:46
  67.4 5.7 %all-to-all-start.1 = ((bf16[1,9,512,128]{3,1,0,2:T(8,128)(2,1)}), bf16[1,9,512,128]{3,1,0,2:T(8,128)(2,1)}, u32[]{:S(2)}, u32[]{:S(2)}) async-start(bf16[1,9,512,128]{3,1,0,2:T(8,128)(2,1)} %copy.131), calls=%async_computation.1 | async-start | bytes 4194304 | tf_op jit(solution)/shard_map/all_to_all | solution.py:60
  78.9 1.8 fusion.128
  84.2 14.2 %all-to-all-done.1 = bf16[1,9,512,128]{3,1,0,2:T(8,128)(2,1)} async-done(((bf16[1,9,512,128]{3,1,0,2:T(8,128)(2,1)}), bf16[1,9,512,128]{3,1,0,2:T(8,128)(2,1)}, u32[]{:S(2)}, u32[]{:S(2)}) %all-to-all-start.1) | async-done | bytes 1179680 | tf_op jit(solution)/shard_map/all_to_all | solution.py:60
  98.4 5.8 %all-to-all-start.3 = ((bf16[1,9,512,128]{3,1,0,2:T(8,128)(2,1)}), bf16[1,9,512,128]{3,1,0,2:T(8,128)(2,1)}, u32[]{:S(2)}, u32[]{:S(2)}) async-start(bf16[1,9,512,128]{3,1,0,2:T(8,128)(2,1)} %copy.134), calls=%async_computation.3 | async-start | bytes 4194304 | tf_op jit(solution)/shard_map/all_to_all | solution.py:60
  104.1 7.1 %fusion.4 = bf16[1024,512]{1,0:T(8,128)(2,1)} fusion(f32[1024,512]{1,0:T(8,128)S(1)} %fusion.123, f32[1024,512]{1,0:T(8,128)} %fusion.124, f32[1024,512]{1,0:T(8,128)} %fusion.125, f32[512,1024]{0,1:T(8,128)} %fusion.126, f32[1024,512]{1,0:T(8,128)} %fusion.127, f32[1024,512]{1,0:T(8,128)} %fusion.128, f32[1024,512]{1,0:T(8,128)} %fusion.130, ...), kind=kOutput, calls=%fused_computation.5 | convolution fusion | flops 138936320 | bytes 18219008 | tf_op jit(solution)/shard_map/bpo,bco->bpc/dot_general | solution.py:33
  111.3 1.9 copy.184
  114.9 1.8 copy.136
  116.7 12.7 %all-to-all-done.3 = bf16[1,9,512,128]{3,1,0,2:T(8,128)(2,1)} async-done(((bf16[1,9,512,128]{3,1,0,2:T(8,128)(2,1)}), bf16[1,9,512,128]{3,1,0,2:T(8,128)(2,1)}, u32[]{:S(2)}, u32[]{:S(2)}) %all-to-all-start.3) | async-done | bytes 1179680 | tf_op jit(solution)/shard_map/all_to_all | solution.py:60
  129.4 1.9 copy.183
  133.0 1.8 copy.137
  137.2 43.6 %all-reduce.4 = (f32[8,8]{1,0:T(8,128)S(1)}, f32[8,8]{1,0:T(8,128)S(1)}) all-reduce(f32[8,8]{1,0:T(8,128)S(1)} %fusion.158, f32[8,8]{1,0:T(8,128)S(1)} %fusion.159), channel_id=1, replica_groups=mesh['batch'=8,'chan'=4] {'batch','chan'}, use_global_device_ids=true, to_apply=%region_1.2 | all-reduce | flops 128 | bytes 1024 | tf_op jit(solution)/shard_map/psum | solution.py:92
  182.0 1.8 subtract_multiply_fusion
  (119 shorter events, 45.0 us)
Async XLA Ops:
  7.2 2.1 %copy-start.22 = (f32[8,8]{1,0:T(8,128)S(1)}, f32[8,8]{1,0:T(8,128)}, u32[]{:S(2)}) copy-start(f32[8,8]{1,0:T(8,128)} %param.11) | copy-start | bytes 772
  18.6 4.4 %copy-start.3 = (bf16[1,32,32,128]{3,2,1,0:T(8,128)(2,1)S(1)}, bf16[1,32,32,128]{3,2,1,0:T(8,128)(2,1)}, u32[]{:S(2)}) copy-start(bf16[1,32,32,128]{3,2,1,0:T(8,128)(2,1)} %param.9) | copy-start | bytes 786436
  18.6 29.1 %all-to-all-start = ((bf16[8,1,9,64,128]{4,3,2,1,0:T(8,128)(2,1)}), bf16[8,1,9,64,128]{4,3,2,1,0:T(8,128)(2,1)S(1)}, u32[]{:S(2)}, u32[]{:S(2)}) async-start(bf16[8,1,9,64,128]{4,3,2,1,0:T(8,128)(2,1)} %bitcast_dynamic-update-slice_fusion.8), calls=%async_computation | async-start | bytes 2359296 | tf_op jit(solution)/shard_map/all_to_all | solution.py:46
  22.9 1.8 copy-start.1
  26.7 3.4 %copy-start.24 = (bf16[1,32,32,512]{3,2,1,0:T(8,128)(2,1)S(1)}, bf16[1,32,32,512]{3,2,1,0:T(8,128)(2,1)}, u32[]{:S(2)}) copy-start(bf16[1,32,32,512]{3,2,1,0:T(8,128)(2,1)} %param.8) | copy-start | bytes 3145732
  35.0 2.2 %copy-start.12 = (bf16[1,16,16,128]{3,2,1,0:T(8,128)(2,1)S(1)}, bf16[1,16,16,128]{3,2,1,0:T(8,128)(2,1)}, u32[]{:S(2)}) copy-start(bf16[1,16,16,128]{3,2,1,0:T(8,128)(2,1)} %param.13) | copy-start | bytes 196612
  35.0 2.2 %copy-start.25 = (bf16[1,16,16,512]{3,2,1,0:T(8,128)(2,1)S(1)}, bf16[1,16,16,512]{3,2,1,0:T(8,128)(2,1)}, u32[]{:S(2)}) copy-start(bf16[1,16,16,512]{3,2,1,0:T(8,128)(2,1)} %param.12) | copy-start | bytes 786436
  47.6 19.7 %all-to-all-start.2 = ((bf16[8,1,9,64,128]{4,3,2,1,0:T(8,128)(2,1)}), bf16[8,1,9,64,128]{4,3,2,1,0:T(8,128)(2,1)}, u32[]{:S(2)}, u32[]{:S(2)}) async-start(bf16[8,1,9,64,128]{4,3,2,1,0:T(8,128)(2,1)} %bitcast_dynamic-update-slice_fusion), calls=%async_computation.2 | async-start | bytes 2359296 | tf_op jit(solution)/shard_map/all_to_all | solution.py:46
  52.1 1.0 copy-start.11
  53.0 0.9 copy-start.10
  54.0 1.8 copy-start.9
  55.7 1.8 copy-start.4
  57.5 1.8 copy-start.8
  67.4 31.0 %all-to-all-start.1 = ((bf16[1,9,512,128]{3,1,0,2:T(8,128)(2,1)}), bf16[1,9,512,128]{3,1,0,2:T(8,128)(2,1)}, u32[]{:S(2)}, u32[]{:S(2)}) async-start(bf16[1,9,512,128]{3,1,0,2:T(8,128)(2,1)} %copy.131), calls=%async_computation.1 | async-start | bytes 4194304 | tf_op jit(solution)/shard_map/all_to_all | solution.py:60
  73.1 1.4 copy-start.20
  73.1 1.7 copy-start.19
  74.8 0.8 copy-start.17
  77.3 1.5 copy-start.7
  78.9 1.8 copy-start.6
  80.7 1.7 copy-start.5
  98.4 31.0 %all-to-all-start.3 = ((bf16[1,9,512,128]{3,1,0,2:T(8,128)(2,1)}), bf16[1,9,512,128]{3,1,0,2:T(8,128)(2,1)}, u32[]{:S(2)}, u32[]{:S(2)}) async-start(bf16[1,9,512,128]{3,1,0,2:T(8,128)(2,1)} %copy.134), calls=%async_computation.3 | async-start | bytes 4194304 | tf_op jit(solution)/shard_map/all_to_all | solution.py:60
  104.1 79.7 %all-reduce.8.cloned.1.call-start = ((), (), s32[]{:S(2)}) async-start(), calls=%async_computation.4 | async-start | bytes 2621440 | tf_op jit(solution)/shard_map/psum | solution.py:57
  133.0 1.8 copy-start
  134.8 1.3 copy-start.2
  (7 other events, 5.8 us)
Sparse Core Ops, SparseCore 0:
  111.4 62.1 all-reduce.7
